TPU v7x, 32 devices: a whole 2x2x4 slice. The times are simulated.
32 devices in a mesh: row: 4 (over z), col: 8 (over y, x, core).
Axes of the slice: x: 2, y: 2, z: 4, core: 2. Of those that a mesh axis runs over, the one named last changes fastest.
Arguments:
- tokens: bfloat16 [512, 8192], P('col', 'row'), may hold values from -6 to 6
- w_gate: bfloat16 [8192, 16384], P('row', 'col'), may hold values from -0.09375 to 0.09375
- w_up: bfloat16 [8192, 16384], P('row', 'col'), may hold values from -0.09375 to 0.09375
- w_down: bfloat16 [16384, 8192], P('col', 'row'), may hold values from -0.0625 to 0.0625
- mask_in: int32 [64, 32], P('col', 'row'), may hold values 0 or 1
- mask_out: int32 [64, 32], P('col', 'row'), may hold values 0 or 1
- out_grad: bfloat16 [512, 8192], P('col', 'row'), may hold values from -6 to 6
Outputs:
- output: bfloat16 [512, 8192], P('col', 'row')
- tokens_grad: bfloat16 [512, 8192], P('col', 'row')
- gate_wgrad: bfloat16 [8192, 16384], P('row', 'col')
- up_wgrad: bfloat16 [8192, 16384], P('row', 'col')
- down_wgrad: bfloat16 [16384, 8192], P('col', 'row')
All inputs are finite; a program needn't handle non-finite values. No bound on the sum of `mask_in` or of `mask_out` on one device may be relied on, other than what follows from the above.
Results may differ from a plain program's by a relative error of at most 0.0049.
Values may be sent and summed in bfloat16 or wider, within the bound.
A program may use at most 128 MiB of HBM per device.

v0:
```python
import jax
import jax.numpy as jnp
from jax import lax
from jax.sharding import PartitionSpec as P

BLOCK = 256


def spread(mask_tile):
    return jnp.repeat(jnp.repeat(mask_tile.T, BLOCK, axis=0), BLOCK, axis=1)


def transposed_right(left, right):
    return lax.dot_general(
        left, right, (((1,), (1,)), ((), ())), preferred_element_type=jnp.float32
    )


def transposed_left(left, right):
    return lax.dot_general(
        left, right, (((0,), (0,)), ((), ())), preferred_element_type=jnp.float32
    )


def local(tokens, w_gate, w_up, w_down, mask_in, mask_out, out_grad):
    keep_in = spread(mask_in).astype(jnp.bfloat16)
    keep_out = spread(mask_out).T.astype(jnp.bfloat16)
    gate_masked = w_gate * keep_in
    up_masked = w_up * keep_in
    down_masked = w_down * keep_out
    hidden_width = w_gate.shape[1]
    x_panel = lax.all_gather(tokens, "col", axis=0, tiled=True)
    row_block = x_panel
    gate_part = jnp.dot(row_block, gate_masked, preferred_element_type=jnp.float32)
    up_part = jnp.dot(row_block, up_masked, preferred_element_type=jnp.float32)
    joined = lax.psum_scatter(
        jnp.concatenate([gate_part, up_part], axis=1), "row", scatter_dimension=0, tiled=True
    )
    gate = joined[:, :hidden_width]
    up = joined[:, hidden_width:]
    sigmoid_gate = jax.nn.sigmoid(gate)
    hidden_share = (gate * sigmoid_gate * up).astype(jnp.bfloat16)
    hidden_full = lax.all_gather(hidden_share, "row", axis=0, tiled=True)
    row_block = hidden_full
    output = lax.psum_scatter(
        jnp.dot(row_block, down_masked, preferred_element_type=jnp.float32),
        "col",
        scatter_dimension=0,
        tiled=True,
    ).astype(jnp.bfloat16)
    dy_panel = lax.all_gather(out_grad, "col", axis=0, tiled=True)
    down_wgrad = (transposed_left(hidden_full, dy_panel) * keep_out.astype(jnp.float32)).astype(
        jnp.bfloat16
    )
    row_block = dy_panel
    hidden_grad = lax.psum_scatter(
        transposed_right(row_block, down_masked), "row", scatter_dimension=0, tiled=True
    )
    up_grad = (hidden_grad * gate * sigmoid_gate).astype(jnp.bfloat16)
    gate_grad = (hidden_grad * up * sigmoid_gate * (1.0 + gate * (1.0 - sigmoid_gate))).astype(
        jnp.bfloat16
    )
    gate_full, up_full = (
        lax.all_gather(gate_grad, "row", axis=0, tiled=True),
        lax.all_gather(up_grad, "row", axis=0, tiled=True),
    )
    keep_wide = keep_in.astype(jnp.float32)
    gate_wgrad = (transposed_left(x_panel, gate_full) * keep_wide).astype(jnp.bfloat16)
    up_wgrad = (transposed_left(x_panel, up_full) * keep_wide).astype(jnp.bfloat16)
    tokens_grad = lax.psum_scatter(
        transposed_right(gate_full, gate_masked) + transposed_right(up_full, up_masked),
        "col",
        scatter_dimension=0,
        tiled=True,
    ).astype(jnp.bfloat16)
    return (output, tokens_grad, gate_wgrad, up_wgrad, down_wgrad)


def solution(mesh):
    placed = (
        P("col", "row"),
        P("row", "col"),
        P("row", "col"),
        P("col", "row"),
        P("col", "row"),
        P("col", "row"),
        P("col", "row"),
    )
    return jax.shard_map(
        local,
        mesh=mesh,
        in_specs=placed,
        out_specs=(
            P("col", "row"),
            P("col", "row"),
            P("row", "col"),
            P("row", "col"),
            P("col", "row"),
        ),
        check_vma=False,
    )
```

profile of v0, /device:TPU:0, one launch (start us, length us, event | category | flops | bytes accessed | tf_op | source)
XLA Modules:
  0.0 554.7 jit_solution(6437327898248120053)
XLA Ops:
  7.2 0.0 all-gather.10.cloned.1.call-start
  7.2 0.7 all-gather.10.cloned.1.call-update
  7.9 0.0 all-gather.6.cloned.1.call-start
  7.9 0.7 all-gather.6.cloned.1.call-update
  8.7 0.0 reduce-scatter.9.cloned.1.call-start
  8.7 0.7 convert_bitcast_fusion
  9.4 0.1 copy.15
  9.5 0.1 broadcast_in_dim.14
  9.6 7.3 %bitcast_multiply_fusion.2 = bf16[2048,2048]{1,0:T(8,128)(2,1)} fusion(bf16[2048,2048]{1,0:T(8,128)(2,1)} %param.10, bf16[2048,8]{0,1:T(8,128)(2,1)S(1)} %bitcast.48), kind=kLoop, calls=%fused_computation.7 | loop fusion | flops 4194304 | bytes 16809984 | tf_op jit(solution)/shard_map/mul | solution.py:30
  16.9 23.5 %all-gather.10.cloned.1.call-done = bf16[512,2048]{1,0:T(8,128)(2,1)} async-done(((bf16[64,2048]{1,0:T(8,128)(2,1)}), bf16[512,2048]{1,0:T(8,128)(2,1)}) %all-gather.10.cloned.1.call-update) | async-done | bytes 2097168 | tf_op jit(solution)/shard_map/all_gather | solution.py:51
  40.4 10.5 %convolution_bitcast_fusion = f32[512,2048]{0,1:T(8,128)} fusion(bf16[2048,2048]{1,0:T(8,128)(2,1)} %bitcast_multiply_fusion.2, bf16[512,2048]{1,0:T(8,128)(2,1)} %all-gather.10.cloned.1.call-done), kind=kOutput, calls=%fused_computation.9 | convolution fusion | flops 4294967296 | bytes 14680064 | tf_op jit(solution)/shard_map/dot_general | solution.py:14
  50.9 0.0 reduce-scatter.9.cloned.1.call-update
  50.9 0.2 reduce-scatter.5.cloned.1.call-start
  51.2 0.4 copy-done.2
  51.6 0.1 copy.12
  51.7 12.2 %copy.13 = bf16[2048,2048]{0,1:T(8,128)(2,1)} copy(bf16[2048,2048]{1,0:T(8,128)(2,1)} %param.8) | data formatting | bytes 16777216 | tf_op args[1]
  63.9 12.2 %copy.14 = bf16[2048,2048]{0,1:T(8,128)(2,1)} copy(bf16[2048,2048]{1,0:T(8,128)(2,1)} %param.9) | data formatting | bytes 16777216 | tf_op args[2]
  76.2 0.1 broadcast_in_dim.12
  76.2 13.7 %bitcast_multiply_fusion.1 = (bf16[2048,2048]{0,1:T(8,128)(2,1)}, bf16[2048,2048]{0,1:T(8,128)(2,1)}) fusion(bf16[2048,2048]{0,1:T(8,128)(2,1)} %copy.13, bf16[2048,8]{0,1:T(8,128)(2,1)S(1)} %bitcast.50, bf16[2048,2048]{0,1:T(8,128)(2,1)} %copy.14), kind=kLoop, calls=%fused_computation.3 | loop fusion | flops 8388608 | bytes 33587200 | tf_op jit(solution)/shard_map/mul | solution.py:28
  89.9 7.8 %convolution_bitcast_fusion.1 = f32[512,2048]{0,1:T(8,128)S(1)} fusion(bf16[2048,2048]{0,1:T(8,128)(2,1)} %get-tuple-element.14, bf16[512,2048]{1,0:T(8,128)(2,1)} %all-gather.6.cloned.1.call-done), kind=kOutput, calls=%fused_computation.10 | convolution fusion | flops 4294967296 | bytes 14680064 | tf_op jit(solution)/shard_map/dot_general | solution.py:35
  97.7 4.8 convolution_bitcast_fusion.2
  102.5 4.2 pad_maximum_fusion
  106.8 0.0 reduce-scatter.5.cloned.1.call-update
  106.8 0.0 all-gather.12.cloned.1.call-start
  106.8 42.4 %reduce-scatter.9.cloned.1.call-done = f32[128,2048]{0,1:T(8,128)} async-done(((f32[512,2048]{0,1:T(8,128)}), f32[128,2048]{0,1:T(8,128)}) %reduce-scatter.9.cloned.1.call-update) | async-done | bytes 1048592 | tf_op jit(solution)/shard_map/reduce_scatter | solution.py:56
  149.2 147.4 %reduce-scatter.5.cloned.1.call-done = f32[128,4096]{0,1:T(8,128)} async-done(((f32[512,4096]{0,1:T(8,128)}), f32[128,4096]{0,1:T(8,128)}) %reduce-scatter.5.cloned.1.call-update) | async-done | bytes 2097168 | tf_op jit(solution)/shard_map/reduce_scatter | solution.py:36
  296.6 3.5 multiply_convert_fusion.1
  300.1 0.0 all-gather.12.cloned.1.call-update
  300.1 0.0 all-gather.14.cloned.1.call-start
  300.2 0.5 all-gather.14.cloned.1.call-update
  300.7 0.0 all-gather.8.cloned.1.call-start
  300.7 0.7 all-gather.8.cloned.1.call-update
  301.4 0.3 reduce-scatter.11.cloned.1.call-start
  301.7 45.4 %all-gather.12.cloned.1.call-done = bf16[512,2048]{0,1:T(8,128)(2,1)} async-done(((bf16[128,2048]{0,1:T(8,128)(2,1)}), bf16[512,2048]{0,1:T(8,128)(2,1)}) %all-gather.12.cloned.1.call-update) | async-done | bytes 2097168 | tf_op jit(solution)/shard_map/all_gather | solution.py:64
  347.1 10.6 %fusion.3 = f32[512,2048]{1,0:T(8,128)} fusion(bf16[512,2048]{0,1:T(8,128)(2,1)} %all-gather.12.cloned.1.call-done, bf16[2048,2048]{0,1:T(8,128)(2,1)} %get-tuple-element.13), kind=kOutput, calls=%fused_computation.20 | convolution fusion | flops 4294967296 | bytes 14680064 | tf_op jit(solution)/shard_map/dot_general | solution.py:14
  357.7 35.3 %all-gather.14.cloned.1.call-done = bf16[512,2048]{0,1:T(8,128)(2,1)} async-done(((bf16[128,2048]{0,1:T(8,128)(2,1)}), bf16[512,2048]{0,1:T(8,128)(2,1)}) %all-gather.14.cloned.1.call-update) | async-done | bytes 2097168 | tf_op jit(solution)/shard_map/all_gather | solution.py:65
  393.0 11.7 %convolution_add_fusion = f32[512,2048]{1,0:T(8,128)} fusion(f32[512,2048]{1,0:T(8,128)} %fusion.3, bf16[512,2048]{0,1:T(8,128)(2,1)} %all-gather.14.cloned.1.call-done, bf16[2048,2048]{0,1:T(8,128)(2,1)} %get-tuple-element.14), kind=kOutput, calls=%fused_computation.12 | convolution fusion | flops 4296015872 | bytes 18874368 | tf_op jit(solution)/shard_map/dot_general | solution.py:14
  404.8 0.3 reduce-scatter.7.cloned.1.call-start
  405.1 34.0 %all-gather.8.cloned.1.call-done = bf16[512,2048]{0,1:T(8,128)(2,1)} async-done(((bf16[128,2048]{0,1:T(8,128)(2,1)}), bf16[512,2048]{0,1:T(8,128)(2,1)}) %all-gather.8.cloned.1.call-update) | async-done | bytes 2097168 | tf_op jit(solution)/shard_map/all_gather | solution.py:43
  439.1 10.5 %fusion.2 = f32[512,2048]{1,0:T(8,128)} fusion(bf16[512,2048]{0,1:T(8,128)(2,1)} %all-gather.8.cloned.1.call-done, bf16[2048,2048]{1,0:T(8,128)(2,1)} %bitcast_multiply_fusion.2), kind=kOutput, calls=%fused_computation.19 | convolution fusion | flops 4294967296 | bytes 14680064 | tf_op jit(solution)/shard_map/dot_general | solution.py:46
  449.6 8.5 %fusion = bf16[2048,2048]{0,1:T(8,128)(2,1)} fusion(bf16[512,2048]{0,1:T(8,128)(2,1)} %all-gather.12.cloned.1.call-done, bf16[512,2048]{1,0:T(8,128)(2,1)S(1)} %copy-done.4, bf16[2048,8]{0,1:T(8,128)(2,1)S(1)} %bitcast.51), kind=kOutput, calls=%fused_computation.4 | convolution fusion | flops 4307550208 | bytes 12615680 | tf_op jit(solution)/shard_map/dot_general | solution.py:20
  458.1 12.0 %copy.16 = bf16[2048,2048]{1,0:T(8,128)(2,1)} copy(bf16[2048,2048]{0,1:T(8,128)(2,1)} %fusion) | data formatting | bytes 16777216
  470.1 8.3 %fusion.1 = bf16[2048,2048]{0,1:T(8,128)(2,1)} fusion(bf16[512,2048]{0,1:T(8,128)(2,1)S(1)} %copy-done.1, bf16[512,2048]{1,0:T(8,128)(2,1)} %all-gather.6.cloned.1.call-done, bf16[2048,8]{0,1:T(8,128)(2,1)S(1)} %bitcast.52), kind=kOutput, calls=%fused_computation.5 | convolution fusion | flops 4307550208 | bytes 12615680 | tf_op jit(solution)/shard_map/dot_general | solution.py:20
  478.4 12.4 %copy.17 = bf16[2048,2048]{1,0:T(8,128)(2,1)} copy(bf16[2048,2048]{0,1:T(8,128)(2,1)} %fusion.1) | data formatting | bytes 16777216
  490.8 8.4 %multiply_convert_fusion = bf16[2048,2048]{1,0:T(8,128)(2,1)} fusion(bf16[512,2048]{0,1:T(8,128)(2,1)} %all-gather.8.cloned.1.call-done, bf16[512,2048]{1,0:T(8,128)(2,1)S(1)} %copy-done.3, bf16[2048,8]{0,1:T(8,128)(2,1)S(1)} %bitcast.49), kind=kOutput, calls=%fused_computation.6 | convolution fusion | flops 4307550208 | bytes 12615680 | tf_op jit(solution)/shard_map/dot_general | solution.py:20
  499.2 1.8 convert_element_type.74
  501.0 45.4 %reduce-scatter.7.cloned.1.call-done = f32[64,2048]{1,0:T(8,128)} async-done(((f32[512,2048]{1,0:T(8,128)}), f32[64,2048]{1,0:T(8,128)}) %reduce-scatter.7.cloned.1.call-update) | async-done | bytes 524304 | tf_op jit(solution)/shard_map/reduce_scatter | solution.py:45
  546.4 1.8 convert_element_type.71
  (14 shorter events, 0.1 us)
Async XLA Ops:
  7.2 33.2 %all-gather.10.cloned.1.call-start = ((), (), s32[]{:S(2)}) async-start(), calls=%async_computation.8 | async-start | bytes 2359296 | tf_op jit(solution)/shard_map/all_gather | solution.py:51
  7.9 82.0 %all-gather.6.cloned.1.call-start = ((), (), s32[]{:S(2)}) async-start(), calls=%async_computation.4 | async-start | bytes 2359296 | tf_op jit(solution)/shard_map/all_gather | solution.py:32
  8.7 140.6 %reduce-scatter.9.cloned.1.call-start = ((), (), s32[]{:S(2)}) async-start(), calls=%async_computation.9 | async-start | bytes 5242880 | tf_op jit(solution)/shard_map/reduce_scatter | solution.py:56
  50.9 0.7 copy-start.2
  50.9 245.6 %reduce-scatter.5.cloned.1.call-start = ((), (), s32[]{:S(2)}) async-start(), calls=%async_computation.5 | async-start | bytes 10485760 | tf_op jit(solution)/shard_map/reduce_scatter | solution.py:36
  89.9 7.8 %copy-start = (bf16[2048,2048]{0,1:T(8,128)(2,1)S(1)}, bf16[2048,2048]{0,1:T(8,128)(2,1)}, u32[]{:S(2)}) copy-start(bf16[2048,2048]{0,1:T(8,128)(2,1)} %get-tuple-element.13) | copy-start | bytes 25165828
  89.9 7.8 %copy-start.4 = (bf16[512,2048]{1,0:T(8,128)(2,1)S(1)}, bf16[512,2048]{1,0:T(8,128)(2,1)}, u32[]{:S(2)}) copy-start(bf16[512,2048]{1,0:T(8,128)(2,1)} %all-gather.6.cloned.1.call-done) | copy-start | bytes 6291460
  106.8 240.4 %all-gather.12.cloned.1.call-start = ((), (), s32[]{:S(2)}) async-start(), calls=%async_computation.10 | async-start | bytes 2621440 | tf_op jit(solution)/shard_map/all_gather | solution.py:64
  300.1 92.9 %all-gather.14.cloned.1.call-start = ((), (), s32[]{:S(2)}) async-start(), calls=%async_computation.11 | async-start | bytes 2621440 | tf_op jit(solution)/shard_map/all_gather | solution.py:65
  300.7 138.4 %all-gather.8.cloned.1.call-start = ((), (), s32[]{:S(2)}) async-start(), calls=%async_computation.6 | async-start | bytes 2621440 | tf_op jit(solution)/shard_map/all_gather | solution.py:43
  301.4 197.7 %reduce-scatter.11.cloned.1.call-start = ((), (), s32[]{:S(2)}) async-start(), calls=%async_computation.12 | async-start | bytes 4718592 | tf_op jit(solution)/shard_map/reduce_scatter | solution.py:70
  404.8 141.6 %reduce-scatter.7.cloned.1.call-start = ((), (), s32[]{:S(2)}) async-start(), calls=%async_computation.7 | async-start | bytes 4718592 | tf_op jit(solution)/shard_map/reduce_scatter | solution.py:45
  458.1 12.0 %copy-start.1 = (bf16[512,2048]{0,1:T(8,128)(2,1)S(1)}, bf16[512,2048]{0,1:T(8,128)(2,1)}, u32[]{:S(2)}) copy-start(bf16[512,2048]{0,1:T(8,128)(2,1)} %all-gather.14.cloned.1.call-done) | copy-start | bytes 6291460
  478.4 12.4 %copy-start.3 = (bf16[512,2048]{1,0:T(8,128)(2,1)S(1)}, bf16[512,2048]{1,0:T(8,128)(2,1)}, u32[]{:S(2)}) copy-start(bf16[512,2048]{1,0:T(8,128)(2,1)} %all-gather.10.cloned.1.call-done) | copy-start | bytes 6291460
Sparse Core Ops, SparseCore 0:
  9.9 30.4 all-gather.9
  42.3 27.7 all-gather.5
  72.4 76.7 reduce-scatter.8
  151.4 145.1 reduce-scatter.4
  300.2 46.8 all-gather.11
  348.6 44.4 all-gather.13
  394.6 44.4 all-gather.7
  442.4 49.3 reduce-scatter.10
  495.2 51.1 reduce-scatter.6
where the time goes:
time: 556 us; the launch traced here: 555 us
  waiting for transfers between devices  376 us (68%)
  matrix products  81.1 us (15%)
  local copies, waits for them, and re-layouts  49.6 us (9%)
  other arithmetic  33 us (6%)
  between operations  13.9 us (2%)
    reduce_scatter x1, waiting for transfers between devices, local(): lax.psum_scatter(jnp.concatenate([gate_part, up_part], axis=1), 'row', sc...  147 us
    unnamed x14, local copies, waits for them, and re-layouts  49.3 us
    all_gather x1, waiting for transfers between devices, local(): lax.all_gather(gate_grad, 'row', axis=0, tiled=True)  45.4 us
    reduce_scatter x1, waiting for transfers between devices, local(): lax.psum_scatter(jnp.dot(row_block, down_masked, preferred_element_type=j...  45.4 us
    reduce_scatter x1, waiting for transfers between devices, local(): lax.psum_scatter(transposed_right(row_block, down_masked), 'row', scatter...  42.4 us
    all_gather x1, waiting for transfers between devices, local(): lax.all_gather(up_grad, 'row', axis=0, tiled=True)  35.3 us
    all_gather x1, waiting for transfers between devices, local(): hidden_full = lax.all_gather(hidden_share, 'row', axis=0, tiled=True)  34 us
    dot_general x3, matrix products, transposed_right(): lax.dot_general(left, right, (((1,), (1,)), ((), ())), preferred_element_...  32.8 us
  transfers between devices with their start and end apart: 9, of which 7 were waited for; matrix products, arithmetic and copies ran while one was open for 28% of the time, Pallas kernels for 0%

commit v1 on v0

--- a/solution.py
+++ b/solution.py
@@ -40,7 +40,12 @@
     up = joined[:, hidden_width:]
     sigmoid_gate = jax.nn.sigmoid(gate)
     hidden_share = (gate * sigmoid_gate * up).astype(jnp.bfloat16)
-    hidden_full = lax.all_gather(hidden_share, "row", axis=0, tiled=True)
+    ring = [hidden_share]
+    for hop in range(3):
+        ring.append(lax.ppermute(ring[-1], "row", [(dev, (dev + 1) % 4) for dev in range(4)]))
+    hidden_full = jnp.roll(
+        jnp.concatenate(ring[::-1], axis=0), (lax.axis_index("row") + 1) * ring[0].shape[0], axis=0
+    )
     row_block = hidden_full
     output = lax.psum_scatter(
         jnp.dot(row_block, down_masked, preferred_element_type=jnp.float32),

time: 556 us -> 527 us (0.948)
  waiting for transfers between devices: 376 us -> 328 us
  starting transfers between devices: 1.02 us -> 17 us
    ppermute x0 -> x3, waiting for transfers between devices: none -> 54.8 us  [local(): lax.ppermute(ring[-1], 'row', [(dev, (dev + 1) % 4) for dev in range(4)])]
    reduce_scatter x1, waiting for transfers between devices: 45.4 us -> 0.01 us  [local(): lax.psum_scatter(jnp.dot(row_block, down_masked, preferred_element_type=j...]
    all_gather x1, waiting for transfers between devices: 45.4 us -> 0.02 us  [local(): lax.all_gather(gate_grad, 'row', axis=0, tiled=True)]
    reduce_scatter x1, waiting for transfers between devices: 0.01 us -> 43.7 us  [local(): lax.psum_scatter(transposed_right(gate_full, gate_masked) + transposed_ri...]
    all_gather x1 -> x0, waiting for transfers between devices: 34 us -> none  [local(): hidden_full = lax.all_gather(hidden_share, 'row', axis=0, tiled=True)]
    all_gather x1, waiting for transfers between devices: 35.3 us -> 14.9 us  [local(): lax.all_gather(up_grad, 'row', axis=0, tiled=True)]
    ppermute x0 -> x3, starting transfers between devices: none -> 16.3 us  [local(): lax.ppermute(ring[-1], 'row', [(dev, (dev + 1) % 4) for dev in range(4)])]
    unnamed x14 -> x27, local copies, waits for them, and re-layouts: 49.3 us -> 54.5 us
  transfers between devices with their start and end apart: 9 -> 11, of which waited for: 7 -> 8; matrix products, arithmetic and copies ran while one was open for 28% -> 30% of each run, Pallas kernels for 0% -> 0%
where the time goes in v1:
time: 527 us; the launch traced here: 526 us
  waiting for transfers between devices  328 us (62%)
  matrix products  78.6 us (15%)
  local copies, waits for them, and re-layouts  55 us (10%)
  other arithmetic  32.9 us (6%)
  starting transfers between devices  17 us (3%)
  between operations  14.3 us (3%)
    reduce_scatter x1, waiting for transfers between devices, local(): lax.psum_scatter(jnp.concatenate([gate_part, up_part], axis=1), 'row', sc...  147 us
    ppermute x3, waiting for transfers between devices, local(): lax.ppermute(ring[-1], 'row', [(dev, (dev + 1) % 4) for dev in range(4)])  54.8 us
    unnamed x27, local copies, waits for them, and re-layouts  54.5 us
    reduce_scatter x1, waiting for transfers between devices, local(): lax.psum_scatter(transposed_right(gate_full, gate_masked) + transposed_ri...  43.7 us
    reduce_scatter x1, waiting for transfers between devices, local(): lax.psum_scatter(transposed_right(row_block, down_masked), 'row', scatter...  42.4 us
    dot_general x3, matrix products, transposed_right(): lax.dot_general(left, right, (((1,), (1,)), ((), ())), preferred_element_...  32.8 us
    dot_general x3, matrix products, transposed_left(): lax.dot_general(left, right, (((0,), (0,)), ((), ())), preferred_element_...  23.7 us
    all_gather x1, waiting for transfers between devices, local(): dy_panel = lax.all_gather(out_grad, 'col', axis=0, tiled=True)  23.5 us
  transfers between devices with their start and end apart: 11, of which 8 were waited for; matrix products, arithmetic and copies ran while one was open for 30% of the time, Pallas kernels for 0%

profile of v1, /device:TPU:0, one launch (start us, length us, event | category | flops | bytes accessed | tf_op | source)
XLA Modules:
  0.0 525.9 jit_solution(6620633989236931014)
XLA Ops:
  7.2 0.7 all-gather.7.cloned.1.call-update
  7.9 0.7 all-gather.5.cloned.1.call-update
  8.7 0.7 convert_bitcast_fusion
  9.4 0.1 copy.15
  9.6 7.3 %bitcast_multiply_fusion.2 = bf16[2048,2048]{1,0:T(8,128)(2,1)} fusion(bf16[2048,2048]{1,0:T(8,128)(2,1)} %param.10, bf16[2048,8]{0,1:T(8,128)(2,1)S(1)} %bitcast.46), kind=kLoop, calls=%fused_computation.7 | loop fusion | flops 4194304 | bytes 16809984 | tf_op jit(solution)/shard_map/mul | solution.py:30
  16.9 23.5 %all-gather.7.cloned.1.call-done = bf16[512,2048]{1,0:T(8,128)(2,1)} async-done(((bf16[64,2048]{1,0:T(8,128)(2,1)}), bf16[512,2048]{1,0:T(8,128)(2,1)}) %all-gather.7.cloned.1.call-update) | async-done | bytes 2097168 | tf_op jit(solution)/shard_map/all_gather | solution.py:56
  40.4 10.5 %convolution_bitcast_fusion = f32[512,2048]{0,1:T(8,128)} fusion(bf16[2048,2048]{1,0:T(8,128)(2,1)} %bitcast_multiply_fusion.2, bf16[512,2048]{1,0:T(8,128)(2,1)} %all-gather.7.cloned.1.call-done), kind=kOutput, calls=%fused_computation.9 | convolution fusion | flops 4294967296 | bytes 14680064 | tf_op jit(solution)/shard_map/dot_general | solution.py:14
  50.9 0.2 reduce-scatter.5.cloned.1.call-start
  51.2 0.4 copy-done.3
  51.6 0.1 copy.12
  51.7 12.2 %copy.13 = bf16[2048,2048]{0,1:T(8,128)(2,1)} copy(bf16[2048,2048]{1,0:T(8,128)(2,1)} %param.8) | data formatting | bytes 16777216 | tf_op args[1]
  63.9 12.2 %copy.14 = bf16[2048,2048]{0,1:T(8,128)(2,1)} copy(bf16[2048,2048]{1,0:T(8,128)(2,1)} %param.9) | data formatting | bytes 16777216 | tf_op args[2]
  76.2 13.7 %bitcast_multiply_fusion.1 = (bf16[2048,2048]{0,1:T(8,128)(2,1)}, bf16[2048,2048]{0,1:T(8,128)(2,1)}) fusion(bf16[2048,2048]{0,1:T(8,128)(2,1)} %copy.13, bf16[2048,8]{0,1:T(8,128)(2,1)S(1)} %bitcast.48, bf16[2048,2048]{0,1:T(8,128)(2,1)} %copy.14), kind=kLoop, calls=%fused_computation.3 | loop fusion | flops 8388608 | bytes 33587200 | tf_op jit(solution)/shard_map/mul | solution.py:28
  89.9 7.8 %convolution_bitcast_fusion.1 = f32[512,2048]{0,1:T(8,128)S(1)} fusion(bf16[2048,2048]{0,1:T(8,128)(2,1)} %get-tuple-element.14, bf16[512,2048]{1,0:T(8,128)(2,1)} %all-gather.5.cloned.1.call-done), kind=kOutput, calls=%fused_computation.10 | convolution fusion | flops 4294967296 | bytes 14680064 | tf_op jit(solution)/shard_map/dot_general | solution.py:35
  97.7 4.8 convolution_bitcast_fusion.2
  102.5 4.2 pad_maximum_fusion
  106.8 42.4 %reduce-scatter.9.cloned.1.call-done = f32[128,2048]{0,1:T(8,128)} async-done(((f32[512,2048]{0,1:T(8,128)}), f32[128,2048]{0,1:T(8,128)}) %reduce-scatter.9.cloned.1.call-update) | async-done | bytes 1048592 | tf_op jit(solution)/shard_map/reduce_scatter | solution.py:61
  149.2 147.4 %reduce-scatter.5.cloned.1.call-done = f32[128,4096]{0,1:T(8,128)} async-done(((f32[512,4096]{0,1:T(8,128)}), f32[128,4096]{0,1:T(8,128)}) %reduce-scatter.5.cloned.1.call-update) | async-done | bytes 2097168 | tf_op jit(solution)/shard_map/reduce_scatter | solution.py:36
  296.6 3.4 multiply_convert_fusion.1
  300.1 1.1 collective-permute-start
  301.2 17.8 %collective-permute-done = bf16[128,2048]{0,1:T(8,128)(2,1)S(1)} collective-permute-done((bf16[128,2048]{0,1:T(8,128)(2,1)S(1)}, bf16[128,2048]{0,1:T(8,128)(2,1)S(1)}, u32[]{:S(2)}, u32[]{:S(2)}) %collective-permute-start) | collective-permute-done | bytes 524320 | tf_op jit(solution)/shard_map/ppermute | solution.py:45
  319.0 6.7 %collective-permute-start.1 = (bf16[128,2048]{0,1:T(8,128)(2,1)S(1)}, bf16[128,2048]{0,1:T(8,128)(2,1)S(1)}, u32[]{:S(2)}, u32[]{:S(2)}) collective-permute-start(bf16[128,2048]{0,1:T(8,128)(2,1)S(1)} %collective-permute-done), channel_id=1, source_target_pairs={{0,8},{8,16},{16,24},{24,0},{1,9},{9,17},{17,25},{25,1},{2,10},{10... | collective-permute-start | bytes 1572872 | tf_op jit(solution)/shard_map/ppermute | solution.py:45
  325.7 22.1 %collective-permute-done.1 = bf16[128,2048]{0,1:T(8,128)(2,1)S(1)} collective-permute-done((bf16[128,2048]{0,1:T(8,128)(2,1)S(1)}, bf16[128,2048]{0,1:T(8,128)(2,1)S(1)}, u32[]{:S(2)}, u32[]{:S(2)}) %collective-permute-start.1) | collective-permute-done | bytes 524320 | tf_op jit(solution)/shard_map/ppermute | solution.py:45
  347.8 8.5 %collective-permute-start.2 = (bf16[128,2048]{0,1:T(8,128)(2,1)S(1)}, bf16[128,2048]{0,1:T(8,128)(2,1)S(1)}, u32[]{:S(2)}, u32[]{:S(2)}) collective-permute-start(bf16[128,2048]{0,1:T(8,128)(2,1)S(1)} %collective-permute-done.1), channel_id=1, source_target_pairs={{0,8},{8,16},{16,24},{24,0},{1,9},{9,17},{17,25},{25,1},{2,10},{10... | collective-permute-start | bytes 1572872 | tf_op jit(solution)/shard_map/ppermute | solution.py:45
  356.4 0.3 reduce-scatter.7.cloned.1.call-start
  356.7 14.8 %collective-permute-done.2 = bf16[128,2048]{0,1:T(8,128)(2,1)S(1)} collective-permute-done((bf16[128,2048]{0,1:T(8,128)(2,1)S(1)}, bf16[128,2048]{0,1:T(8,128)(2,1)S(1)}, u32[]{:S(2)}, u32[]{:S(2)}) %collective-permute-start.2) | collective-permute-done | bytes 524320 | tf_op jit(solution)/shard_map/ppermute | solution.py:45
  371.5 0.1 constant_dynamic-update-slice_fusion.7
  371.6 0.2 constant_dynamic-update-slice_fusion.6
  371.8 0.2 constant_dynamic-update-slice_fusion.5
  372.0 0.2 constant_dynamic-update-slice_fusion.4
  372.2 0.2 constant_dynamic-update-slice_fusion.3
  372.4 0.2 constant_dynamic-update-slice_fusion.2
  372.6 0.2 constant_dynamic-update-slice_fusion.1
  372.8 0.2 constant_dynamic-update-slice_fusion
  373.0 1.9 copy-done.2
  374.9 9.5 %fusion.3 = f32[512,2048]{1,0:T(8,128)} fusion(bf16[2048,2048]{1,0:T(8,128)(2,1)} %bitcast_multiply_fusion.2, bf16[1024,2048]{0,1:T(8,128)(2,1)S(1)} %constant_dynamic-update-slice_fusion, s32[]{:T(128)S(6)} %select_n.14), kind=kOutput, calls=%fused_computation.14 | convolution fusion | flops 4294967296 | bytes 14680068 | tf_op jit(solution)/shard_map/dot_general | solution.py:51
  384.5 10.6 %fusion.7 = f32[512,2048]{1,0:T(8,128)} fusion(bf16[512,2048]{0,1:T(8,128)(2,1)} %all-gather.9.cloned.1.call-done, bf16[2048,2048]{0,1:T(8,128)(2,1)} %get-tuple-element.13), kind=kOutput, calls=%fused_computation.32 | convolution fusion | flops 4294967296 | bytes 14680064 | tf_op jit(solution)/shard_map/dot_general | solution.py:14
  395.1 14.9 %all-gather.11.cloned.1.call-done = bf16[512,2048]{0,1:T(8,128)(2,1)} async-done(((bf16[128,2048]{0,1:T(8,128)(2,1)}), bf16[512,2048]{0,1:T(8,128)(2,1)}) %all-gather.11.cloned.1.call-update) | async-done | bytes 2097168 | tf_op jit(solution)/shard_map/all_gather | solution.py:70
  410.0 11.7 %convolution_add_fusion = f32[512,2048]{1,0:T(8,128)} fusion(f32[512,2048]{1,0:T(8,128)} %fusion.7, bf16[512,2048]{0,1:T(8,128)(2,1)} %all-gather.11.cloned.1.call-done, bf16[2048,2048]{0,1:T(8,128)(2,1)} %get-tuple-element.14), kind=kOutput, calls=%fused_computation.12 | convolution fusion | flops 4296015872 | bytes 18874368 | tf_op jit(solution)/shard_map/dot_general | solution.py:14
  421.7 1.8 copy-done.6
  423.5 8.6 %multiply_convert_fusion = bf16[2048,2048]{1,0:T(8,128)(2,1)} fusion(bf16[512,2048]{1,0:T(8,128)(2,1)S(1)} %copy-done.6, bf16[2048,8]{0,1:T(8,128)(2,1)S(1)} %bitcast.47, bf16[1024,2048]{0,1:T(8,128)(2,1)} %copy-done.2, s32[]{:T(128)S(6)} %select_n.14), kind=kOutput, calls=%fused_computation.6 | convolution fusion | flops 4307550208 | bytes 12615684 | tf_op jit(solution)/shard_map/dot_general | solution.py:20
  432.1 6.8 %fusion = bf16[2048,2048]{0,1:T(8,128)(2,1)} fusion(bf16[512,2048]{0,1:T(8,128)(2,1)S(1)} %copy-done.7, bf16[512,2048]{1,0:T(8,128)(2,1)S(1)} %copy-done.5, bf16[2048,8]{0,1:T(8,128)(2,1)S(1)} %bitcast.49), kind=kOutput, calls=%fused_computation.4 | convolution fusion | flops 4307550208 | bytes 12615680 | tf_op jit(solution)/shard_map/dot_general | solution.py:20
  438.9 12.4 %copy.16 = bf16[2048,2048]{1,0:T(8,128)(2,1)} copy(bf16[2048,2048]{0,1:T(8,128)(2,1)} %fusion) | data formatting | bytes 16777216
  451.3 8.3 %fusion.1 = bf16[2048,2048]{0,1:T(8,128)(2,1)} fusion(bf16[512,2048]{0,1:T(8,128)(2,1)S(1)} %copy-done.1, bf16[512,2048]{1,0:T(8,128)(2,1)} %all-gather.5.cloned.1.call-done, bf16[2048,8]{0,1:T(8,128)(2,1)S(1)} %bitcast.50), kind=kOutput, calls=%fused_computation.5 | convolution fusion | flops 4307550208 | bytes 12615680 | tf_op jit(solution)/shard_map/dot_general | solution.py:20
  459.6 12.3 %copy.17 = bf16[2048,2048]{1,0:T(8,128)(2,1)} copy(bf16[2048,2048]{0,1:T(8,128)(2,1)} %fusion.1) | data formatting | bytes 16777216
  471.9 1.8 convert_element_type.71
  473.7 43.7 %reduce-scatter.11.cloned.1.call-done = f32[64,2048]{1,0:T(8,128)} async-done(((f32[512,2048]{1,0:T(8,128)}), f32[64,2048]{1,0:T(8,128)}) %reduce-scatter.11.cloned.1.call-update) | async-done | bytes 524304 | tf_op jit(solution)/shard_map/reduce_scatter | solution.py:75
  517.3 1.8 convert_element_type.74
  (31 shorter events, 0.5 us)
Async XLA Ops:
  7.2 33.2 %all-gather.7.cloned.1.call-start = ((), (), s32[]{:S(2)}) async-start(), calls=%async_computation.7 | async-start | bytes 2359296 | tf_op jit(solution)/shard_map/all_gather | solution.py:56
  7.9 82.0 %all-gather.5.cloned.1.call-start = ((), (), s32[]{:S(2)}) async-start(), calls=%async_computation.4 | async-start | bytes 2359296 | tf_op jit(solution)/shard_map/all_gather | solution.py:32
  8.7 140.6 %reduce-scatter.9.cloned.1.call-start = ((), (), s32[]{:S(2)}) async-start(), calls=%async_computation.8 | async-start | bytes 5242880 | tf_op jit(solution)/shard_map/reduce_scatter | solution.py:61
  50.9 0.7 copy-start.3
  50.9 245.6 %reduce-scatter.5.cloned.1.call-start = ((), (), s32[]{:S(2)}) async-start(), calls=%async_computation.5 | async-start | bytes 10485760 | tf_op jit(solution)/shard_map/reduce_scatter | solution.py:36
  89.9 7.8 %copy-start = (bf16[2048,2048]{0,1:T(8,128)(2,1)S(1)}, bf16[2048,2048]{0,1:T(8,128)(2,1)}, u32[]{:S(2)}) copy-start(bf16[2048,2048]{0,1:T(8,128)(2,1)} %get-tuple-element.13) | copy-start | bytes 25165828
  89.9 7.8 %copy-start.4 = (bf16[512,2048]{1,0:T(8,128)(2,1)S(1)}, bf16[512,2048]{1,0:T(8,128)(2,1)}, u32[]{:S(2)}) copy-start(bf16[512,2048]{1,0:T(8,128)(2,1)} %all-gather.5.cloned.1.call-done) | copy-start | bytes 6291460
  106.8 277.7 %all-gather.9.cloned.1.call-start = ((), (), s32[]{:S(2)}) async-start(), calls=%async_computation.9 | async-start | bytes 2621440 | tf_op jit(solution)/shard_map/all_gather | solution.py:69
  300.0 110.0 %all-gather.11.cloned.1.call-start = ((), (), s32[]{:S(2)}) async-start(), calls=%async_computation.10 | async-start | bytes 2621440 | tf_op jit(solution)/shard_map/all_gather | solution.py:70
  300.1 18.9 %collective-permute-start = (bf16[128,2048]{0,1:T(8,128)(2,1)S(1)}, bf16[128,2048]{0,1:T(8,128)(2,1)S(1)}, u32[]{:S(2)}, u32[]{:S(2)}) collective-permute-start(bf16[128,2048]{0,1:T(8,128)(2,1)S(1)} %get-tuple-element.12), channel_id=1, source_target_pairs={{0,8},{8,16},{16,24},{24,0},{1,9},{9,17},{17,25},{25,1},{2,10},{10... | collective-permute-start | bytes 1572872 | tf_op jit(solution)/shard_map/ppermute | solution.py:45
  319.0 28.9 %collective-permute-start.1 = (bf16[128,2048]{0,1:T(8,128)(2,1)S(1)}, bf16[128,2048]{0,1:T(8,128)(2,1)S(1)}, u32[]{:S(2)}, u32[]{:S(2)}) collective-permute-start(bf16[128,2048]{0,1:T(8,128)(2,1)S(1)} %collective-permute-done), channel_id=1, source_target_pairs={{0,8},{8,16},{16,24},{24,0},{1,9},{9,17},{17,25},{25,1},{2,10},{10... | collective-permute-start | bytes 1572872 | tf_op jit(solution)/shard_map/ppermute | solution.py:45
  347.8 23.6 %collective-permute-start.2 = (bf16[128,2048]{0,1:T(8,128)(2,1)S(1)}, bf16[128,2048]{0,1:T(8,128)(2,1)S(1)}, u32[]{:S(2)}, u32[]{:S(2)}) collective-permute-start(bf16[128,2048]{0,1:T(8,128)(2,1)S(1)} %collective-permute-done.1), channel_id=1, source_target_pairs={{0,8},{8,16},{16,24},{24,0},{1,9},{9,17},{17,25},{25,1},{2,10},{10... | collective-permute-start | bytes 1572872 | tf_op jit(solution)/shard_map/ppermute | solution.py:45
  356.4 115.5 %reduce-scatter.7.cloned.1.call-start = ((), (), s32[]{:S(2)}) async-start(), calls=%async_computation.6 | async-start | bytes 4718592 | tf_op jit(solution)/shard_map/reduce_scatter | solution.py:50
  372.9 1.9 copy-start.2
  384.4 132.9 %reduce-scatter.11.cloned.1.call-start = ((), (), s32[]{:S(2)}) async-start(), calls=%async_computation.11 | async-start | bytes 4718592 | tf_op jit(solution)/shard_map/reduce_scatter | solution.py:75
  421.7 1.8 copy-start.6
  423.5 8.6 %copy-start.5 = (bf16[512,2048]{1,0:T(8,128)(2,1)S(1)}, bf16[512,2048]{1,0:T(8,128)(2,1)}, u32[]{:S(2)}) copy-start(bf16[512,2048]{1,0:T(8,128)(2,1)} %all-gather.5.cloned.1.call-done) | copy-start | bytes 6291460
  423.5 8.6 %copy-start.7 = (bf16[512,2048]{0,1:T(8,128)(2,1)S(1)}, bf16[512,2048]{0,1:T(8,128)(2,1)}, u32[]{:S(2)}) copy-start(bf16[512,2048]{0,1:T(8,128)(2,1)} %all-gather.9.cloned.1.call-done) | copy-start | bytes 6291460
  438.9 12.4 %copy-start.1 = (bf16[512,2048]{0,1:T(8,128)(2,1)S(1)}, bf16[512,2048]{0,1:T(8,128)(2,1)}, u32[]{:S(2)}) copy-start(bf16[512,2048]{0,1:T(8,128)(2,1)} %all-gather.11.cloned.1.call-done) | copy-start | bytes 6291460
Sparse Core Ops, SparseCore 0:
  9.9 30.4 all-gather.6
  42.3 27.7 all-gather.4
  72.4 76.7 reduce-scatter.8
  151.4 145.1 reduce-scatter.4
  300.2 63.7 all-gather.8
  365.3 44.6 all-gather.10
  413.4 49.3 reduce-scatter.6
  466.1 51.1 reduce-scatter.10
